TPU v7x, 256 devices: a whole 4x4x8 slice. The times are simulated.
256 devices in a mesh: section: 8 (over x, z_hi), expert: 8 (over z_lo, core), tensor: 4 (over y).
Axes of the slice: x: 4, y: 4, z: 8 (z_hi: 2, z_lo: 4; z = z_hi * 4 + z_lo), core: 2. Of those that a mesh axis runs over, the one named last changes fastest.
Arguments:
- tokens: bfloat16 [512, 6144], P(('section', 'expert'), 'tensor'), may hold values from -6 to 6
- routes: int32 [512, 2], P(('section', 'expert')), may hold values from 0 to 7, all different within a row; in each aligned block of 8 rows (0 to 7, 8 to 15, ...) at most 4 rows name the same one
- router: float32 [6144, 8], replicated, may hold values from -0.18 to 0.18
- gate_proj: bfloat16 [8, 6144, 8192], P('expert', None, ('section', 'tensor')), may hold values from -0.078125 to 0.078125
- up_proj: bfloat16 [8, 6144, 8192], P('expert', None, ('section', 'tensor')), may hold values from -0.078125 to 0.078125
- down_proj: bfloat16 [8, 8192, 6144], P('expert', ('section', 'tensor')), may hold values from -0.125 to 0.125
- grad_out: bfloat16 [512, 6144], P(('section', 'expert'), 'tensor'), may hold values from -6 to 6
Outputs:
- moe_out: bfloat16 [512, 6144], P(('section', 'expert'), 'tensor')
- grad_tokens: bfloat16 [512, 6144], P(('section', 'expert'), 'tensor')
- grad_router: float32 [6144, 8], P('tensor')
Inputs may be any that keep to these rules, and one draw needn't show every extreme that they name: `routes`: each token names 2 different experts; in each aligned block of 8 tokens (the tokens of one group) no expert is named by more than 4 tokens, and in some blocks one expert is named by exactly 4.
All inputs are finite; a program needn't handle non-finite values.
Results may differ from a plain program's by a relative error of at most 0.02.
Values may be sent and summed in bfloat16 or wider, within the bound.
No kernel may reach another device: no remote copies, remote signals or barrier semaphores. Data moves between devices by JAX's collectives and lax.ppermute only.
A program may use at most 64 MiB of HBM per device.

v0:
```python
import jax
import jax.numpy as jnp
from jax import lax
from jax.sharding import PartitionSpec as P

precise = lax.Precision.HIGHEST


def route_table(routes, expert_count, capacity):
    flat_ids = routes.reshape(-1)
    expert_hot = (flat_ids[:, None] == jnp.arange(expert_count, dtype=jnp.int32)[None, :]).astype(
        jnp.float32
    )
    earlier = jnp.cumsum(expert_hot, axis=0) - expert_hot
    slot_ids = jnp.sum(earlier * expert_hot, axis=1).astype(jnp.int32)
    slot_hot = (slot_ids[:, None] == jnp.arange(capacity, dtype=jnp.int32)[None, :]).astype(
        jnp.float32
    )
    routing = expert_hot.T[:, None, :] * slot_hot.T[None, :, :]
    return routing.reshape(expert_count * capacity, flat_ids.shape[0])


def gate_weights(logits, routes):
    chosen = jnp.take_along_axis(logits, routes, axis=1)
    scores = jax.nn.sigmoid(chosen)
    totals = jnp.sum(scores, axis=1, keepdims=True)
    return (scores, scores / totals)


def expert_front(rows_x, gate_mat, up_mat):
    pre_gate = jnp.dot(rows_x, gate_mat, preferred_element_type=jnp.float32)
    pre_up = jnp.dot(rows_x, up_mat, preferred_element_type=jnp.float32)
    gate_sig = jax.nn.sigmoid(pre_gate)
    gate_act = pre_gate * gate_sig
    hidden = (gate_act * pre_up).astype(jnp.bfloat16)
    return (pre_gate, pre_up, gate_sig, gate_act, hidden)


def expert_grads(grad_hidden, pre_gate, pre_up, gate_sig, gate_act):
    grad_gate = (grad_hidden * pre_up * gate_sig * (1.0 + pre_gate * (1.0 - gate_sig))).astype(
        jnp.bfloat16
    )
    grad_up = (grad_hidden * gate_act).astype(jnp.bfloat16)
    return (grad_gate, grad_up)


def router_grads(grad_weight, scores, routes, expert_count):
    totals = scores[:, 0] + scores[:, 1]
    first = (grad_weight[:, 0] - grad_weight[:, 1]) * scores[:, 1] / (totals * totals)
    second = (grad_weight[:, 1] - grad_weight[:, 0]) * scores[:, 0] / (totals * totals)
    grad_scores = jnp.stack([first, second], axis=1)
    grad_chosen = grad_scores * scores * (1.0 - scores)
    expert_hot = (
        routes[:, :, None] == jnp.arange(expert_count, dtype=jnp.int32)[None, None, :]
    ).astype(jnp.float32)
    return jnp.sum(expert_hot * grad_chosen[:, :, None], axis=1)


def contract_last(left, right):
    return lax.dot_general(
        left, right, (((1,), (1,)), ((), ())), preferred_element_type=jnp.float32
    )


def on_device(tokens, routes, router, gate_proj, up_proj, down_proj, grad_out):
    tok_rows, quarter = tokens.shape
    tensor_count = lax.axis_size("tensor")
    expert_count = lax.axis_size("expert")
    top_count = routes.shape[1]
    capacity = 2 * tok_rows * top_count // expert_count
    block_rows = expert_count * capacity
    tensor_index = lax.axis_index("tensor")
    router_rows = lax.dynamic_slice_in_dim(router, tensor_index * quarter, quarter, 0)
    routing = route_table(routes, expert_count, capacity)
    gate_mat = gate_proj[0]
    up_mat = up_proj[0]
    down_mat = down_proj[0]
    send_x, send_dy = (tokens, grad_out)
    logits = lax.psum(jnp.dot(tokens.astype(jnp.float32), router_rows, precision=precise), "tensor")
    scores, weight = gate_weights(logits, routes)
    row_width = send_x.shape[1]
    x_sent = jnp.dot(
        routing, jnp.repeat(send_x.astype(jnp.float32), top_count, axis=0), precision=precise
    )
    x_sent = x_sent.astype(jnp.bfloat16).reshape(expert_count, capacity, row_width)
    scaled = jnp.repeat(send_dy.astype(jnp.float32), top_count, axis=0) * weight.reshape(-1, 1)
    dy_sent = (
        jnp.dot(routing, scaled, precision=precise)
        .astype(jnp.bfloat16)
        .reshape(expert_count, capacity, row_width)
    )

    def block_ids(count):
        return jnp.arange(count // block_rows, dtype=jnp.int32)

    def forward_block(hidden, block):
        section_at = block // tensor_count
        tensor_at = block % tensor_count
        hidden_rows = lax.dynamic_slice_in_dim(hidden, section_at * block_rows, block_rows, 0)
        columns = lax.dynamic_slice_in_dim(down_mat, tensor_at * quarter, quarter, 1)
        return jnp.dot(hidden_rows, columns, preferred_element_type=jnp.float32)

    def backward_block(grad_gate, grad_up, block):
        section_at = block // tensor_count
        tensor_at = block % tensor_count
        gate_rows = lax.dynamic_slice_in_dim(grad_gate, section_at * block_rows, block_rows, 0)
        up_rows = lax.dynamic_slice_in_dim(grad_up, section_at * block_rows, block_rows, 0)
        gate_part = lax.dynamic_slice_in_dim(gate_mat, tensor_at * quarter, quarter, 0)
        up_part = lax.dynamic_slice_in_dim(up_mat, tensor_at * quarter, quarter, 0)
        return contract_last(gate_rows, gate_part) + contract_last(up_rows, up_part)

    landed_x = lax.all_to_all(x_sent, "expert", split_axis=0, concat_axis=0, tiled=True)
    landed_x = lax.all_gather(landed_x, "tensor", axis=2, tiled=True)
    rows_x = lax.all_gather(landed_x.reshape(block_rows, -1), "section", axis=0, tiled=True)
    pre_gate, pre_up, gate_sig, gate_act, hidden = expert_front(rows_x, gate_mat, up_mat)
    summed_out = lax.psum_scatter(
        lax.map(
            lambda block: forward_block(hidden, block),
            block_ids(lax.axis_size(("section", "tensor")) * block_rows),
        )
        .reshape(lax.axis_size(("section", "tensor")) * block_rows, quarter)
        .astype(jnp.bfloat16),
        ("section", "tensor"),
        scatter_dimension=0,
        tiled=True,
    ).astype(jnp.float32)
    expert_out = lax.all_to_all(
        summed_out.reshape(expert_count, capacity, quarter).astype(jnp.bfloat16),
        "expert",
        split_axis=0,
        concat_axis=0,
        tiled=True,
    ).astype(jnp.float32)
    landed_dy = lax.all_to_all(dy_sent, "expert", split_axis=0, concat_axis=0, tiled=True)
    landed_dy = lax.all_gather(landed_dy, "tensor", axis=2, tiled=True)
    rows_dy = lax.all_gather(landed_dy.reshape(block_rows, -1), "section", axis=0, tiled=True)
    grad_hidden = contract_last(rows_dy, down_mat)
    grad_gate, grad_up = expert_grads(grad_hidden, pre_gate, pre_up, gate_sig, gate_act)
    summed_grad = lax.psum_scatter(
        lax.map(
            lambda block: backward_block(grad_gate, grad_up, block),
            block_ids(lax.axis_size(("section", "tensor")) * block_rows),
        )
        .reshape(lax.axis_size(("section", "tensor")) * block_rows, quarter)
        .astype(jnp.bfloat16),
        ("section", "tensor"),
        scatter_dimension=0,
        tiled=True,
    ).astype(jnp.float32)
    expert_grad = lax.all_to_all(
        summed_grad.reshape(expert_count, capacity, quarter).astype(jnp.bfloat16),
        "expert",
        split_axis=0,
        concat_axis=0,
        tiled=True,
    ).astype(jnp.float32)
    out_route = jnp.dot(
        routing.T, expert_out.reshape(block_rows, quarter), precision=precise
    ).reshape(tok_rows, top_count, quarter)
    grad_route = jnp.dot(
        routing.T, expert_grad.reshape(block_rows, quarter), precision=precise
    ).reshape(tok_rows, top_count, quarter)
    moe_out = jnp.sum(weight[:, :, None] * out_route, axis=1).astype(jnp.bfloat16)
    weight_part = jnp.sum(grad_out.astype(jnp.float32)[:, None, :] * out_route, axis=2)
    grad_weight = lax.psum(weight_part, "tensor")
    grad_logits = router_grads(grad_weight, scores, routes, expert_count)
    grad_tokens = (
        jnp.sum(grad_route, axis=1) + jnp.dot(grad_logits, router_rows.T, precision=precise)
    ).astype(jnp.bfloat16)
    router_part = jnp.dot(tokens.astype(jnp.float32).T, grad_logits, precision=precise)
    grad_router = lax.psum(router_part, ("section", "expert"))
    return (moe_out, grad_tokens, grad_router)


def solution(mesh):
    return jax.shard_map(
        on_device,
        mesh=mesh,
        in_specs=(
            P(("section", "expert"), "tensor"),
            P(("section", "expert"), None),
            P(),
            P("expert", None, ("section", "tensor")),
            P("expert", None, ("section", "tensor")),
            P("expert", ("section", "tensor"), None),
            P(("section", "expert"), "tensor"),
        ),
        out_specs=(
            P(("section", "expert"), "tensor"),
            P(("section", "expert"), "tensor"),
            P("tensor", None),
        ),
        check_vma=False,
    )
```

profile of v0, /device:TPU:8, one launch (start us, length us, event | category | flops | bytes accessed | tf_op | source)
XLA Modules:
  0.0 1154.4 jit_solution(11186698686855565210)
XLA Ops:
  9.6 12.0 %all_to_all.20 = bf16[8,4,1536]{2,1,0:T(4,128)(2,1)S(1)} all-to-all(bf16[8,4,1536]{2,1,0:T(4,128)(2,1)S(1)} %reshape.192), channel_id=1, replica_groups=mesh['section'=8,'expert'=8,'tensor'=4] {'expert'}, dimensions={0} | all-to-all | bytes 196608 | tf_op jit(solution)/shard_map/all_to_all | solution.py:112
  21.7 13.1 %all_gather.12 = bf16[8,4,6144]{2,1,0:T(4,128)(2,1)S(1)} all-gather(bf16[8,4,1536]{2,1,0:T(4,128)(2,1)S(1)} %all_to_all.20), channel_id=1, replica_groups=mesh['section'=8,'expert'=8,'tensor'=4] {'tensor'}, dimensions={2}, use_global_device_ids=true | all-gather | bytes 491520 | tf_op jit(solution)/shard_map/all_gather | solution.py:113
  37.5 8.1 psum.21
  47.0 16.7 %all_to_all.21 = bf16[8,4,1536]{2,1,0:T(4,128)(2,1)S(1)} all-to-all(bf16[8,4,1536]{2,1,0:T(4,128)(2,1)S(1)} %reshape.195), channel_id=1, replica_groups=mesh['section'=8,'expert'=8,'tensor'=4] {'expert'}, dimensions={0} | all-to-all | bytes 196608 | tf_op jit(solution)/shard_map/all_to_all | solution.py:134
  63.7 12.4 %all_gather.14 = bf16[8,4,6144]{2,1,0:T(4,128)(2,1)S(1)} all-gather(bf16[8,4,1536]{2,1,0:T(4,128)(2,1)S(1)} %all_to_all.21), channel_id=1, replica_groups=mesh['section'=8,'expert'=8,'tensor'=4] {'tensor'}, dimensions={2}, use_global_device_ids=true | all-gather | bytes 491520 | tf_op jit(solution)/shard_map/all_gather | solution.py:135
  77.1 51.9 %all-gather.3.cloned.1.call-done = bf16[256,6144]{1,0:T(8,128)(2,1)} async-done(((bf16[32,6144]{1,0:T(8,128)(2,1)}), bf16[256,6144]{1,0:T(8,128)(2,1)}) %all-gather.3.cloned.1.call-update) | async-done | bytes 3145744 | tf_op jit(solution)/shard_map/all_gather | solution.py:114
  129.0 4.7 fusion.29
  133.7 1.7 fusion.31
  135.4 83.3 %all-gather.5.cloned.1.call-done = bf16[256,6144]{1,0:T(8,128)(2,1)} async-done(((bf16[32,6144]{1,0:T(8,128)(2,1)}), bf16[256,6144]{1,0:T(8,128)(2,1)}) %all-gather.5.cloned.1.call-update) | async-done | bytes 3145744 | tf_op jit(solution)/shard_map/all_gather | solution.py:136
  218.7 4.6 multiply_convert_fusion
  223.7 147.5 %while.24 = (s32[]{:T(128)}, bf16[32,32,1536]{2,1,0:T(8,128)(2,1)S(1)}, s32[32]{0:T(128)S(1)}, bf16[256,256]{1,0:T(8,128)(2,1)}, bf16[256,6144]{1,0:T(8,128)(2,1...) while((s32[]{:T(128)}, ...), condition=%wide.region_5.6_spmd, body=%wide.region_4.5_spmd.sunk | while | flops 25165852 | bytes 999876 | solution.py:117
  371.1 1.7 copy-done.2
  373.2 198.6 %while.25 = (s32[]{:T(128)}, bf16[32,32,1536]{2,1,0:T(8,128)(2,1)S(1)}, s32[32]{0:T(128)S(1)}, bf16[256,256]{1,0:T(8,128)(2,1)}, bf16[6144,256]{1,0:T(8,128)(2,1...) while((s32[]{:T(128)}, ...), condition=%wide.region_9.10_spmd, body=%wide.region_8.9_spmd.sunk | while | flops 50380828 | bytes 2195932 | solution.py:140
  409.0 1.5 fusion.64
  446.2 1.5 fusion.64
  571.9 1.7 copy-done.1
  573.6 52.4 %reduce-scatter.3.cloned.1.call-done = bf16[32,1536]{1,0:T(8,128)(2,1)} async-done(((bf16[1024,1536]{1,0:T(8,128)(2,1)}), bf16[32,1536]{1,0:T(8,128)(2,1)}) %reduce-scatter.3.cloned.1.call-update) | async-done | bytes 98320 | tf_op jit(solution)/shard_map/reduce_scatter | solution.py:116
  626.0 1.5 convert_element_type.89
  627.5 3.4 all-to-all-start.1
  631.0 253.9 %reduce-scatter.5.cloned.1.call-done = bf16[32,1536]{1,0:T(8,128)(2,1)} async-done(((bf16[1024,1536]{1,0:T(8,128)(2,1)}), bf16[32,1536]{1,0:T(8,128)(2,1)}) %reduce-scatter.5.cloned.1.call-update) | async-done | bytes 98320 | tf_op jit(solution)/shard_map/reduce_scatter | solution.py:139
  884.9 1.6 convert_element_type.97
  886.4 3.4 all-to-all-start.3
  890.6 9.5 psum.22
  900.4 246.4 %psum.23 = f32[1536,8]{0,1:T(8,128)} all-reduce(f32[1536,8]{0,1:T(8,128)S(1)} %convolution_bitcast_fusion.1), channel_id=1, replica_groups=mesh['section'=8,'expert'=8,'tensor'=4] {'section','expert'}, use_global_device_ids=true, to_apply=%region_15.16 | all-reduce | flops 12288 | bytes 98304 | tf_op jit(solution)/shard_map/psum | solution.py:171
  (226 shorter events, 184.9 us)
Async XLA Ops:
  7.2 29.4 %copy-start = (f32[6144,8]{0,1:T(8,128)S(1)}, f32[6144,8]{0,1:T(8,128)}, u32[]{:S(2)}) copy-start(f32[6144,8]{0,1:T(8,128)} %param.13) | copy-start | bytes 589828
  7.2 121.8 %all-gather.3.cloned.1.call-start = ((), (), s32[]{:S(2)}) async-start(), calls=%async_computation.6 | async-start | bytes 3538944 | tf_op jit(solution)/shard_map/all_gather | solution.py:114
  9.6 36.7 %copy-start.5 = (bf16[8,1536]{1,0:T(8,128)(2,1)S(1)}, bf16[8,1536]{1,0:T(8,128)(2,1)}, u32[]{:S(2)}) copy-start(bf16[8,1536]{1,0:T(8,128)(2,1)} %param.17) | copy-start | bytes 73732
  9.6 36.7 %copy-start.6 = (s32[8,2]{0,1:T(2,128)S(1)}, s32[8,2]{0,1:T(2,128)}, u32[]{:S(2)}) copy-start(s32[8,2]{0,1:T(2,128)} %param.12) | copy-start | bytes 196
  35.7 183.0 %all-gather.5.cloned.1.call-start = ((), (), s32[]{:S(2)}) async-start(), calls=%async_computation.8 | async-start | bytes 3538944 | tf_op jit(solution)/shard_map/all_gather | solution.py:136
  77.0 549.0 %reduce-scatter.3.cloned.1.call-start = ((), (), s32[]{:S(2)}) async-start(), calls=%async_computation.7 | async-start | bytes 3244032 | tf_op jit(solution)/shard_map/reduce_scatter | solution.py:116
  77.0 56.6 %copy-start.3 = (bf16[1,6144,256]{2,1,0:T(8,128)(2,1)S(1)}, bf16[1,6144,256]{2,1,0:T(8,128)(2,1)}, u32[]{:S(2)}) copy-start(bf16[1,6144,256]{2,1,0:T(8,128)(2,1)} %param.14) | copy-start | bytes 9437188
  129.0 4.7 copy-start.7
  371.1 1.7 copy-start.2
  372.8 512.0 %reduce-scatter.5.cloned.1.call-start = ((), (), s32[]{:S(2)}) async-start(), calls=%async_computation.9 | async-start | bytes 3244032 | tf_op jit(solution)/shard_map/reduce_scatter | solution.py:139
  571.9 1.7 copy-start.1
  571.9 328.3 %copy-start.4 = (bf16[8,1536]{1,0:T(8,128)(2,1)S(1)}, bf16[8,1536]{1,0:T(8,128)(2,1)}, u32[]{:S(2)}) copy-start(bf16[8,1536]{1,0:T(8,128)(2,1)} %param.11) | copy-start | bytes 73732
  627.5 258.9 %all-to-all-start.1 = ((bf16[8,4,1536]{2,1,0:T(4,128)(2,1)}), bf16[8,4,1536]{2,1,0:T(4,128)(2,1)S(1)}, u32[]{:S(2)}, u32[]{:S(2)}) async-start(bf16[8,4,1536]{2,1,0:T(4,128)(2,1)} %convert_element_type.89), calls=%async_computation.2 | async-start | bytes 196608 | tf_op jit(solution)/shard_map/all_to_all | solution.py:127
  886.4 260.4 %all-to-all-start.3 = ((bf16[8,4,1536]{2,1,0:T(4,128)(2,1)}), bf16[8,4,1536]{2,1,0:T(4,128)(2,1)S(1)}, u32[]{:S(2)}, u32[]{:S(2)}) async-start(bf16[8,4,1536]{2,1,0:T(4,128)(2,1)} %convert_element_type.97), calls=%async_computation.5 | async-start | bytes 196608 | tf_op jit(solution)/shard_map/all_to_all | solution.py:150
Sparse Core Ops, SparseCore 0:
  35.8 93.1 all-gather.2
  131.6 87.0 all-gather.4
  373.0 252.9 reduce-scatter.2
  632.1 252.7 reduce-scatter.4
where the time goes:
time: 1160 us; the launch traced here: 1150 us
  waiting for transfers between devices  442 us (38%)
  blocking collectives  318 us (27%)
  loops' own time  169 us (15%)
  matrix products  154 us (13%)
  local copies, waits for them, and re-layouts  50 us (4%)
  between operations  14 us (1%)
    reduce_scatter x1, waiting for transfers between devices, on_device(): lax.psum_scatter(lax.map(lambda block: backward_block(grad_gate, grad_up,...  254 us
    psum x1, blocking collectives, on_device(): grad_router = lax.psum(router_part, ('section', 'expert'))  246 us
    dot_general x65, matrix products, contract_last(): lax.dot_general(left, right, (((1,), (1,)), ((), ())), preferred_element_...  99.8 us
    another operation x1, loops' own time, on_device(): lax.map(lambda block: backward_block(grad_gate, grad_up, block), block_id...  84.7 us
    another operation x1, loops' own time, on_device(): lax.map(lambda block: forward_block(hidden, block), block_ids(lax.axis_si...  83.9 us
    all_gather x1, waiting for transfers between devices, on_device(): lax.all_gather(landed_dy.reshape(block_rows, -1), 'section', axis=0, tile...  83.3 us
    reduce_scatter x1, waiting for transfers between devices, on_device(): lax.psum_scatter(lax.map(lambda block: forward_block(hidden, block), bloc...  52.4 us
    all_gather x1, waiting for transfers between devices, on_device(): lax.all_gather(landed_x.reshape(block_rows, -1), 'section', axis=0, tiled...  51.9 us
  transfers between devices with their start and end apart: 6, of which 4 were waited for; matrix products, arithmetic and copies ran while one was open for 11% of the time, Pallas kernels for 0%

commit v1 on v0

--- a/solution.py
+++ b/solution.py
@@ -168,7 +168,8 @@
         jnp.sum(grad_route, axis=1) + jnp.dot(grad_logits, router_rows.T, precision=precise)
     ).astype(jnp.bfloat16)
     router_part = jnp.dot(tokens.astype(jnp.float32).T, grad_logits, precision=precise)
-    grad_router = lax.psum(router_part, ("section", "expert"))
+    partial = lax.psum(router_part, "section")
+    grad_router = lax.psum(partial, "expert")
     return (moe_out, grad_tokens, grad_router)
 
 

time: 1160 us -> 993 us (0.86)
  blocking collectives: 318 us -> 148 us
    psum x1 -> x2, blocking collectives: 246 us -> 76.2 us  [the longest x1 49.1 us: on_device(): partial = lax.psum(router_part, 'section')]
  transfers between devices with their start and end apart: 6 -> 6, of which waited for: 4 -> 4; matrix products, arithmetic and copies ran while one was open for 11% -> 13% of each run, Pallas kernels for 0% -> 0%
where the time goes in v1:
time: 993 us; the launch traced here: 984 us
  waiting for transfers between devices  442 us (45%)
  loops' own time  169 us (17%)
  matrix products  154 us (16%)
  blocking collectives  148 us (15%)
  local copies, waits for them, and re-layouts  50 us (5%)
  between operations  14 us (1%)
    reduce_scatter x1, waiting for transfers between devices, on_device(): lax.psum_scatter(lax.map(lambda block: backward_block(grad_gate, grad_up,...  254 us
    dot_general x65, matrix products, contract_last(): lax.dot_general(left, right, (((1,), (1,)), ((), ())), preferred_element_...  99.8 us
    another operation x1, loops' own time, on_device(): lax.map(lambda block: backward_block(grad_gate, grad_up, block), block_id...  84.7 us
    another operation x1, loops' own time, on_device(): lax.map(lambda block: forward_block(hidden, block), block_ids(lax.axis_si...  83.9 us
    all_gather x1, waiting for transfers between devices, on_device(): lax.all_gather(landed_dy.reshape(block_rows, -1), 'section', axis=0, tile...  83.3 us
    reduce_scatter x1, waiting for transfers between devices, on_device(): lax.psum_scatter(lax.map(lambda block: forward_block(hidden, block), bloc...  52.4 us
    all_gather x1, waiting for transfers between devices, on_device(): lax.all_gather(landed_x.reshape(block_rows, -1), 'section', axis=0, tiled...  51.9 us
    psum x1, blocking collectives, on_device(): partial = lax.psum(router_part, 'section')  49.1 us
  transfers between devices with their start and end apart: 6, of which 4 were waited for; matrix products, arithmetic and copies ran while one was open for 13% of the time, Pallas kernels for 0%

profile of v1, /device:TPU:8, one launch (start us, length us, event | category | flops | bytes accessed | tf_op | source)
XLA Modules:
  0.0 984.1 jit_solution(16698983691617334665)
XLA Ops:
  9.6 12.0 %all_to_all.20 = bf16[8,4,1536]{2,1,0:T(4,128)(2,1)S(1)} all-to-all(bf16[8,4,1536]{2,1,0:T(4,128)(2,1)S(1)} %reshape.192), channel_id=1, replica_groups=mesh['section'=8,'expert'=8,'tensor'=4] {'expert'}, dimensions={0} | all-to-all | bytes 196608 | tf_op jit(solution)/shard_map/all_to_all | solution.py:112
  21.7 13.1 %all_gather.12 = bf16[8,4,6144]{2,1,0:T(4,128)(2,1)S(1)} all-gather(bf16[8,4,1536]{2,1,0:T(4,128)(2,1)S(1)} %all_to_all.20), channel_id=1, replica_groups=mesh['section'=8,'expert'=8,'tensor'=4] {'tensor'}, dimensions={2}, use_global_device_ids=true | all-gather | bytes 491520 | tf_op jit(solution)/shard_map/all_gather | solution.py:113
  37.5 8.1 psum.28
  47.0 16.7 %all_to_all.21 = bf16[8,4,1536]{2,1,0:T(4,128)(2,1)S(1)} all-to-all(bf16[8,4,1536]{2,1,0:T(4,128)(2,1)S(1)} %reshape.195), channel_id=1, replica_groups=mesh['section'=8,'expert'=8,'tensor'=4] {'expert'}, dimensions={0} | all-to-all | bytes 196608 | tf_op jit(solution)/shard_map/all_to_all | solution.py:134
  63.7 12.4 %all_gather.14 = bf16[8,4,6144]{2,1,0:T(4,128)(2,1)S(1)} all-gather(bf16[8,4,1536]{2,1,0:T(4,128)(2,1)S(1)} %all_to_all.21), channel_id=1, replica_groups=mesh['section'=8,'expert'=8,'tensor'=4] {'tensor'}, dimensions={2}, use_global_device_ids=true | all-gather | bytes 491520 | tf_op jit(solution)/shard_map/all_gather | solution.py:135
  77.1 51.9 %all-gather.3.cloned.1.call-done = bf16[256,6144]{1,0:T(8,128)(2,1)} async-done(((bf16[32,6144]{1,0:T(8,128)(2,1)}), bf16[256,6144]{1,0:T(8,128)(2,1)}) %all-gather.3.cloned.1.call-update) | async-done | bytes 3145744 | tf_op jit(solution)/shard_map/all_gather | solution.py:114
  129.0 4.7 fusion.29
  133.7 1.7 fusion.31
  135.4 83.3 %all-gather.5.cloned.1.call-done = bf16[256,6144]{1,0:T(8,128)(2,1)} async-done(((bf16[32,6144]{1,0:T(8,128)(2,1)}), bf16[256,6144]{1,0:T(8,128)(2,1)}) %all-gather.5.cloned.1.call-update) | async-done | bytes 3145744 | tf_op jit(solution)/shard_map/all_gather | solution.py:136
  218.7 4.6 multiply_convert_fusion
  223.7 147.5 %while.24 = (s32[]{:T(128)}, bf16[32,32,1536]{2,1,0:T(8,128)(2,1)S(1)}, s32[32]{0:T(128)S(1)}, bf16[256,256]{1,0:T(8,128)(2,1)}, bf16[256,6144]{1,0:T(8,128)(2,1...) while((s32[]{:T(128)}, ...), condition=%wide.region_5.6_spmd, body=%wide.region_4.5_spmd.sunk | while | flops 25165852 | bytes 999876 | solution.py:117
  371.1 1.7 copy-done.2
  373.2 198.6 %while.25 = (s32[]{:T(128)}, bf16[32,32,1536]{2,1,0:T(8,128)(2,1)S(1)}, s32[32]{0:T(128)S(1)}, bf16[256,256]{1,0:T(8,128)(2,1)}, bf16[6144,256]{1,0:T(8,128)(2,1...) while((s32[]{:T(128)}, ...), condition=%wide.region_9.10_spmd, body=%wide.region_8.9_spmd.sunk | while | flops 50380828 | bytes 2195932 | solution.py:140
  446.2 1.5 fusion.64
  571.9 1.7 copy-done.1
  573.6 52.4 %reduce-scatter.3.cloned.1.call-done = bf16[32,1536]{1,0:T(8,128)(2,1)} async-done(((bf16[1024,1536]{1,0:T(8,128)(2,1)}), bf16[32,1536]{1,0:T(8,128)(2,1)}) %reduce-scatter.3.cloned.1.call-update) | async-done | bytes 98320 | tf_op jit(solution)/shard_map/reduce_scatter | solution.py:116
  626.0 1.5 convert_element_type.89
  627.5 3.4 all-to-all-start.1
  631.0 253.9 %reduce-scatter.5.cloned.1.call-done = bf16[32,1536]{1,0:T(8,128)(2,1)} async-done(((bf16[1024,1536]{1,0:T(8,128)(2,1)}), bf16[32,1536]{1,0:T(8,128)(2,1)}) %reduce-scatter.5.cloned.1.call-update) | async-done | bytes 98320 | tf_op jit(solution)/shard_map/reduce_scatter | solution.py:139
  884.9 1.6 convert_element_type.97
  886.4 3.4 all-to-all-start.3
  890.6 9.5 psum.29
  900.4 49.1 %psum.30 = f32[1536,8]{0,1:T(8,128)S(1)} all-reduce(f32[1536,8]{0,1:T(8,128)S(1)} %convolution_bitcast_fusion.1), channel_id=1, replica_groups=mesh['section'=8,'expert'=8,'tensor'=4] {'section'}, use_global_device_ids=true, to_apply=%region_15.16 | all-reduce | flops 12288 | bytes 98304 | tf_op jit(solution)/shard_map/psum | solution.py:171
  949.5 27.1 %psum.31 = f32[1536,8]{0,1:T(8,128)} all-reduce(f32[1536,8]{0,1:T(8,128)S(1)} %psum.30), channel_id=1, replica_groups=mesh['section'=8,'expert'=8,'tensor'=4] {'expert'}, use_global_device_ids=true, to_apply=%region_16.17 | all-reduce | flops 12288 | bytes 98304 | tf_op jit(solution)/shard_map/psum | solution.py:172
  (227 shorter events, 186.4 us)
Async XLA Ops:
  7.2 29.4 %copy-start = (f32[6144,8]{0,1:T(8,128)S(1)}, f32[6144,8]{0,1:T(8,128)}, u32[]{:S(2)}) copy-start(f32[6144,8]{0,1:T(8,128)} %param.13) | copy-start | bytes 589828
  7.2 121.8 %all-gather.3.cloned.1.call-start = ((), (), s32[]{:S(2)}) async-start(), calls=%async_computation.6 | async-start | bytes 3538944 | tf_op jit(solution)/shard_map/all_gather | solution.py:114
  9.6 36.7 %copy-start.5 = (bf16[8,1536]{1,0:T(8,128)(2,1)S(1)}, bf16[8,1536]{1,0:T(8,128)(2,1)}, u32[]{:S(2)}) copy-start(bf16[8,1536]{1,0:T(8,128)(2,1)} %param.17) | copy-start | bytes 73732
  9.6 36.7 %copy-start.6 = (s32[8,2]{0,1:T(2,128)S(1)}, s32[8,2]{0,1:T(2,128)}, u32[]{:S(2)}) copy-start(s32[8,2]{0,1:T(2,128)} %param.12) | copy-start | bytes 196
  35.7 183.0 %all-gather.5.cloned.1.call-start = ((), (), s32[]{:S(2)}) async-start(), calls=%async_computation.8 | async-start | bytes 3538944 | tf_op jit(solution)/shard_map/all_gather | solution.py:136
  77.0 549.0 %reduce-scatter.3.cloned.1.call-start = ((), (), s32[]{:S(2)}) async-start(), calls=%async_computation.7 | async-start | bytes 3244032 | tf_op jit(solution)/shard_map/reduce_scatter | solution.py:116
  77.0 56.6 %copy-start.3 = (bf16[1,6144,256]{2,1,0:T(8,128)(2,1)S(1)}, bf16[1,6144,256]{2,1,0:T(8,128)(2,1)}, u32[]{:S(2)}) copy-start(bf16[1,6144,256]{2,1,0:T(8,128)(2,1)} %param.14) | copy-start | bytes 9437188
  129.0 4.7 copy-start.7
  371.1 1.7 copy-start.2
  372.8 512.0 %reduce-scatter.5.cloned.1.call-start = ((), (), s32[]{:S(2)}) async-start(), calls=%async_computation.9 | async-start | bytes 3244032 | tf_op jit(solution)/shard_map/reduce_scatter | solution.py:139
  571.9 1.7 copy-start.1
  571.9 328.3 %copy-start.4 = (bf16[8,1536]{1,0:T(8,128)(2,1)S(1)}, bf16[8,1536]{1,0:T(8,128)(2,1)}, u32[]{:S(2)}) copy-start(bf16[8,1536]{1,0:T(8,128)(2,1)} %param.11) | copy-start | bytes 73732
  627.5 258.9 %all-to-all-start.1 = ((bf16[8,4,1536]{2,1,0:T(4,128)(2,1)}), bf16[8,4,1536]{2,1,0:T(4,128)(2,1)S(1)}, u32[]{:S(2)}, u32[]{:S(2)}) async-start(bf16[8,4,1536]{2,1,0:T(4,128)(2,1)} %convert_element_type.89), calls=%async_computation.2 | async-start | bytes 196608 | tf_op jit(solution)/shard_map/all_to_all | solution.py:127
  886.4 90.2 %all-to-all-start.3 = ((bf16[8,4,1536]{2,1,0:T(4,128)(2,1)}), bf16[8,4,1536]{2,1,0:T(4,128)(2,1)S(1)}, u32[]{:S(2)}, u32[]{:S(2)}) async-start(bf16[8,4,1536]{2,1,0:T(4,128)(2,1)} %convert_element_type.97), calls=%async_computation.5 | async-start | bytes 196608 | tf_op jit(solution)/shard_map/all_to_all | solution.py:150
Sparse Core Ops, SparseCore 0:
  35.8 93.1 all-gather.2
  131.6 87.0 all-gather.4
  373.0 252.9 reduce-scatter.2
  632.1 252.7 reduce-scatter.4
